TPU v7x, 32 devices: a whole 2x2x4 slice. The times are simulated.
32 devices in a mesh: seq: 16 (over z, y, x), tp: 2 (over core).
Axes of the slice: x: 2, y: 2, z: 4, core: 2. Of those that a mesh axis runs over, the one named last changes fastest.
Arguments:
- queries: bfloat16 [8192, 4096], P('seq', 'tp'), may hold values from -9 to 9
- keys: bfloat16 [8192, 4096], P('seq', 'tp'), may hold values from -9 to 9
- values: bfloat16 [8192, 4096], P('seq', 'tp'), may hold values from -6 to 6
- route: int32 [32, 8192], P('tp', 'seq'), may hold values from 0 to 8191, as said below
- members: int32 [32, 8192], P('tp', 'seq'), may hold values from 0 to 8191, as said below
- pattern: int32 [32, 32, 10], P('tp', 'seq'), may hold values from 0 to 1, as said below
- w_out: bfloat16 [4096, 4096], P('tp', 'seq'), may hold values from -0.125 to 0.125
Outputs:
- mixed: bfloat16 [8192, 4096], P('seq', 'tp')
Inputs may be any that keep to these rules, and one draw needn't show every extreme that they name: `route`: each row is a permutation of the positions; for every aligned block of 512 positions and every aligned block of 512 slots, exactly 32 of the block's positions have their slot in that slot block. members[h] is the inverse permutation of route[h]: members[h, route[h, p]] = p. `pattern`: entries 2 * 2 and 2 * 2 + 1 (the cluster's own blocks) are always 1; entries whose cluster lies outside 0 to 31 are always 0.
All inputs are finite; a program needn't handle non-finite values.
Results may differ from a plain program's by a relative error of at most 0.017.
Values may be sent and summed in bfloat16 or wider, within the bound.
No kernel may reach another device: no remote copies, remote signals or barrier semaphores. Data moves between devices by JAX's collectives and lax.ppermute only.
A program may use at most 128 MiB of HBM per device.

v0:
```python
import jax
import jax.numpy as jnp
from jax import lax
from jax.experimental import pallas as pl
from jax.experimental.pallas import tpu as pltpu
from jax.sharding import PartitionSpec as P


CLUSTER = 256
REACH = 2


def extended_2(cells, sides, width):
    for axis, dim in sides:
        count = lax.axis_size(axis)
        ends = count - 1
        head = lax.slice_in_dim(cells, 0, width, axis=dim)
        tail = lax.slice_in_dim(cells, cells.shape[dim] - width, cells.shape[dim], axis=dim)
        cells = jnp.concatenate(
            [
                lax.ppermute(tail, axis, [(i, (i + 1) % count) for i in range(ends)]),
                cells,
                lax.ppermute(head, axis, [((i + 1) % count, i) for i in range(ends)]),
            ],
            axis=dim,
        )
    return cells


def attend_head(pieces):
    query_rows, key_rows, value_rows, pattern_rows = pieces
    head_width = query_rows.shape[1]
    cluster_count = query_rows.shape[0] // CLUSTER
    window_rows = (2 * REACH + 1) * CLUSTER
    starts = jnp.arange(cluster_count) * CLUSTER
    key_window = jax.vmap(
        lambda slot_start: lax.dynamic_slice_in_dim(key_rows, slot_start, window_rows, 0)
    )(starts)
    value_window = jax.vmap(
        lambda slot_start: lax.dynamic_slice_in_dim(value_rows, slot_start, window_rows, 0)
    )(starts)
    query_blocks = query_rows.reshape(cluster_count, CLUSTER, head_width)
    scores = jnp.einsum(
        "cqd,ckd->cqk", query_blocks, key_window, preferred_element_type=jnp.float32
    ) * head_width ** (-0.5)
    allowed = jnp.repeat(pattern_rows, CLUSTER // 2, axis=1) > 0
    scores = jnp.where(allowed[:, None, :], scores, -jnp.inf)
    row_max = jnp.max(scores, axis=-1, keepdims=True)
    exponent = jnp.exp(scores - row_max)
    weights = (exponent / jnp.sum(exponent, axis=-1, keepdims=True)).astype(jnp.bfloat16)
    context = jnp.einsum(
        "cqk,ckd->cqd", weights, value_window, preferred_element_type=jnp.float32
    ).astype(jnp.bfloat16)
    return context.reshape(query_rows.shape[0], head_width)


def buffer_index(group_of, order_key, per_peer):
    same_group = group_of[:, :, None] == group_of[:, None, :]
    earlier = order_key[:, None, :] < order_key[:, :, None]
    rank = jnp.sum((same_group & earlier).astype(jnp.int32), axis=2)
    return group_of * per_peer + rank


def slot_shards(queries, keys, values, route, members, pattern, w_out):
    rows_here = queries.shape[0]
    head_count = route.shape[0]
    head_width = queries.shape[1] // head_count
    peer_count = lax.axis_size("seq")
    per_peer = rows_here // peer_count
    local_iota = jnp.arange(rows_here, dtype=jnp.int32)
    send_index = buffer_index(route // rows_here, route, per_peer)
    local_slots = jnp.broadcast_to(local_iota[None, :], members.shape)
    arrival_index = buffer_index(members // rows_here, local_slots, per_peer)
    send_table = (send_index[:, None, :] == local_iota[None, :, None]).astype(jnp.bfloat16)
    land_table = (arrival_index[:, :, None] == local_iota[None, None, :]).astype(jnp.bfloat16)
    stacked = jnp.concatenate(
        [
            queries.reshape(rows_here, head_count, head_width),
            keys.reshape(rows_here, head_count, head_width),
            values.reshape(rows_here, head_count, head_width),
        ],
        axis=2,
    )
    packed = jnp.einsum(
        "hap,phd->had", send_table, stacked, preferred_element_type=jnp.float32
    ).astype(jnp.bfloat16)

    def outgoing(column_index):
        part_rows = packed[:, :, column_index * head_width : (column_index + 1) * head_width]
        return part_rows.reshape(head_count, peer_count, per_peer, head_width)

    sent_query, sent_key, sent_value = (
        lax.all_to_all(outgoing(0), "seq", split_axis=1, concat_axis=1, tiled=True),
        lax.all_to_all(outgoing(1), "seq", split_axis=1, concat_axis=1, tiled=True),
        lax.all_to_all(outgoing(2), "seq", split_axis=1, concat_axis=1, tiled=True),
    )
    arrived = jnp.concatenate(
        [
            sent_query.reshape(head_count, rows_here, head_width),
            sent_key.reshape(head_count, rows_here, head_width),
            sent_value.reshape(head_count, rows_here, head_width),
        ],
        axis=2,
    )
    placed = jnp.einsum(
        "hsa,had->hsd", land_table, arrived, preferred_element_type=jnp.float32
    ).astype(jnp.bfloat16)
    ordered_query = placed[:, :, :head_width]
    keys_values = jnp.stack(
        [placed[:, :, head_width : 2 * head_width], placed[:, :, 2 * head_width :]]
    )
    extended = extended_2(keys_values, (("seq", 2),), REACH * CLUSTER)
    context = lax.map(attend_head, (ordered_query, extended[0], extended[1], pattern))
    returning = jnp.einsum(
        "hsa,hsd->had", land_table, context, preferred_element_type=jnp.float32
    ).astype(jnp.bfloat16)
    returning = returning.reshape(head_count, peer_count, per_peer, head_width)
    returned = lax.all_to_all(returning, "seq", split_axis=1, concat_axis=1, tiled=True).reshape(
        head_count, rows_here, head_width
    )
    attended = jnp.einsum(
        "hap,had->phd", send_table, returned, preferred_element_type=jnp.float32
    ).astype(jnp.bfloat16)
    attended = attended.reshape(rows_here, head_count * head_width)
    partial_value = jnp.dot(
        attended,
        lax.all_gather(w_out, "seq", axis=1, tiled=True),
        preferred_element_type=jnp.float32,
    )
    mixed_out = lax.psum_scatter(
        partial_value.astype(jnp.bfloat16), "tp", scatter_dimension=1, tiled=True
    )
    return mixed_out


LANES = 128
DIGIT = 4
TAIL = 16
BLOCK = 128


def order_of(key_row):
    n = key_row.shape[1]
    key_col = jnp.broadcast_to(key_row, (LANES, n)).T
    counts = []
    for j in range(n // LANES):
        less = key_col < key_row[:, j * LANES : (j + 1) * LANES]
        counts.append(jnp.sum(jnp.where(less, 1, 0), axis=0, keepdims=True))
    return jnp.concatenate(counts, axis=1)


def table_to(order_row, first, last):
    n = order_row.shape[1]
    rows = lax.broadcasted_iota(jnp.int32, (last - first, n), 0) + first
    return jnp.where(rows == order_row, 1.0, 0.0).astype(jnp.bfloat16)


def table_from(order_row, first, last):
    n = order_row.shape[1]
    order_col = jnp.broadcast_to(order_row, (LANES, n)).T
    parts = []
    for start in range(first, last, LANES):
        lane = lax.broadcasted_iota(jnp.int32, (n, min(LANES, last - start)), 1) + start
        parts.append(jnp.where(order_col[:, : lane.shape[1]] == lane, 1.0, 0.0).astype(jnp.bfloat16))
    return jnp.concatenate(parts, axis=1) if len(parts) > 1 else parts[0]


def mm(a, b):
    return jnp.dot(a, b, preferred_element_type=jnp.float32)


def pack(route, pattern, queries, keys, values, first, last, order=None):
    heads, rows = route.shape
    width = queries.shape[1] // heads
    lines = rows // LANES
    leads = order is None
    part = last - first
    group = 2

    def emit(i, order_row, refs, out_ref):
        stacked = jnp.concatenate([ref[:, i * width : (i + 1) * width] for ref in refs], axis=1)
        put = mm(table_to(order_row, first, last), stacked).astype(jnp.bfloat16)
        for n in range(3):
            out_ref[i, n * part : (n + 1) * part] = put[:, n * width : (n + 1) * width]

    def lead(route_ref, pat_ref, q_ref, k_ref, v_ref, out_ref, order_ref):
        for i in range(group):
            h = pl.program_id(0) * group + i
            row = route_ref[pl.ds(h, 1), :]
            order_row = order_of(row)
            order_ref[i] = order_row
            emit(i, order_row, (q_ref, k_ref, v_ref), out_ref)
            slot = jnp.bitwise_and(row, rows - 1)
            high = lax.shift_right_logical(slot, DIGIT)
            low = jnp.bitwise_and(slot, (1 << DIGIT) - 1)
            at = lax.broadcasted_iota(jnp.int32, (8, rows), 0)
            digits = jnp.where(at == 0, high, jnp.where(at == 1, low, 0))
            digits = digits.astype(jnp.float32).astype(jnp.bfloat16)
            sorted_digits = lax.dot_general(
                digits,
                table_to(order_row, 0, rows),
                (((1,), (1,)), ((), ())),
                preferred_element_type=jnp.float32,
            )
            parts = [
                sorted_digits[d : d + 1, j * LANES : (j + 1) * LANES]
                for d in range(2)
                for j in range(lines)
            ]
            parts.append(pat_ref[pl.ds(h, 1), :].astype(jnp.float32))
            parts.append(jnp.zeros((TAIL - 2 * lines - 1, LANES), jnp.float32))
            out_ref[i, 3 * part :] = jnp.concatenate(parts, axis=0).astype(jnp.bfloat16)

    def follow(order_ref, q_ref, k_ref, v_ref, out_ref):
        for i in range(group):
            emit(i, order_ref[i], (q_ref, k_ref, v_ref), out_ref)

    columns = pl.BlockSpec((rows, group * width), lambda h: (0, h))
    order_spec = pl.BlockSpec((group, 1, rows), lambda h: (h, 0, 0))
    total = 3 * part + (TAIL if leads else 0)
    out_spec = pl.BlockSpec((group, total, width), lambda h: (h, 0, 0))
    out_shape = jax.ShapeDtypeStruct((heads, total, width), jnp.bfloat16)
    if not leads:
        return pl.pallas_call(
            follow,
            name="pack_rest",
            grid=(heads // group,),
            in_specs=[order_spec, columns, columns, columns],
            out_specs=out_spec,
            out_shape=out_shape,
        )(order, queries, keys, values)
    return pl.pallas_call(
        lead,
        name="pack",
        grid=(heads // group,),
        in_specs=[
            pl.BlockSpec((heads, rows), lambda h: (0, 0)),
            pl.BlockSpec((heads, LANES), lambda h: (0, 0)),
            columns,
            columns,
            columns,
        ],
        out_specs=[out_spec, order_spec],
        out_shape=[out_shape, jax.ShapeDtypeStruct((heads, 1, rows), jnp.int32)],
    )(route, pattern, queries, keys, values)


def tail_of(arrived, rows, entries):
    senders = arrived.shape[0]
    lines = rows // LANES
    tail = arrived[:, -TAIL:].astype(jnp.int32)
    slot = (tail[:, :lines] << DIGIT) + tail[:, lines : 2 * lines]
    slot = slot.reshape(senders, senders, rows // senders).transpose(1, 0, 2)
    return slot.reshape(senders, rows), tail[:, 2 * lines, :entries].reshape(-1)


def attend(slots, pattern, arrived, count, kept=None):
    nb, rows = slots.shape
    senders, _, width = arrived.shape
    per = rows // senders
    per_block = rows // CLUSTER
    window = (2 * REACH + 1) * CLUSTER
    blocks = window // BLOCK
    leads = kept is None
    lowest = 0 if leads else nb - count
    steps = count if leads else count + 1
    done = count - 1 if leads else count + 1
    ahead = rows if leads else 2 * rows
    total = (count + (1 if leads else 3)) * rows
    scale = width ** (-0.5) * 1.4426950408889634

    def kernel(pat_ref, slot_ref, q_ref, k_ref, v_ref, *refs):
        if leads:
            out_ref, q_keep, k_keep, v_keep, kbuf, vbuf, qbuf = refs
        else:
            q_kept, k_kept, v_kept, out_ref, kbuf, vbuf, qbuf = refs
        g = pl.program_id(0)

        @pl.when(g == 0)
        def _():
            zero = jnp.zeros((rows, width), jnp.bfloat16)
            vbuf[:, width:] = jnp.ones((total, width), jnp.bfloat16)
            if leads:
                kbuf[:rows, :] = zero
                vbuf[:rows, :width] = zero
            else:
                kbuf[: 2 * rows, :] = k_kept[...]
                vbuf[: 2 * rows, :width] = v_kept[...]
                qbuf[(lowest - 1) % 2] = q_kept[...]
                kbuf[total - rows :, :] = zero
                vbuf[total - rows :, :width] = zero

        @pl.when(g < count)
        def _():
            block = g + lowest
            table = table_to(slot_ref[pl.ds(block, 1), :], 0, rows)
            at = pl.multiple_of(g * rows + ahead, rows)
            put = [
                mm(table, ref[...].reshape(rows, width)).astype(jnp.bfloat16)
                for ref in (q_ref, k_ref, v_ref)
            ]
            qbuf[pl.ds(block % 2, 1)] = put[0][None]
            kbuf[pl.ds(at, rows), :] = put[1]
            vbuf[pl.ds(at, rows), :width] = put[2]
            if leads:

                @pl.when(g == count - 1)
                def _():
                    q_keep[...] = put[0]
                    k_keep[:rows, :] = kbuf[total - 2 * rows : total - rows, :]
                    v_keep[:rows, :] = vbuf[total - 2 * rows : total - rows, :width]
                    k_keep[rows:, :] = put[1]
                    v_keep[rows:, :] = put[2]

        @pl.when(g + lowest > 0)
        def _():
            b = g + lowest - 1
            base = (g - 1 if leads else g) * rows
            contexts = []
            for i in range(per_block):
                q = qbuf[pl.ds(b % 2, 1), i * CLUSTER : (i + 1) * CLUSTER, :][0]
                at = pl.multiple_of(base + i * CLUSTER, CLUSTER)
                scores = lax.dot_general(
                    q,
                    kbuf[pl.ds(at, window), :],
                    (((1,), (1,)), ((), ())),
                    preferred_element_type=jnp.float32,
                )
                parts = []
                for j in range(blocks):
                    allowed = pat_ref[(b * per_block + i) * blocks + j] > 0
                    shift = jnp.where(allowed, 0.0, -jnp.inf)
                    parts.append(scores[:, j * BLOCK : (j + 1) * BLOCK] + shift)
                most = parts[0]
                for part in parts[1:]:
                    most = jnp.maximum(most, part)
                most = jnp.max(most, axis=1, keepdims=True)
                weights = jnp.concatenate(
                    [jnp.exp2((part - most) * scale).astype(jnp.bfloat16) for part in parts], axis=1
                )
                both = mm(weights, vbuf[pl.ds(at, window), :])
                contexts.append((both[:, :width] / both[:, width:]).astype(jnp.bfloat16))
            context = jnp.concatenate(contexts, axis=0)
            back = mm(table_from(slot_ref[pl.ds(b, 1), :], 0, rows), context).astype(jnp.bfloat16)
            out_ref[...] = back.reshape(senders, per, width)

    whole = lambda *shape: pl.BlockSpec(shape, lambda g, p: (0,) * len(shape))
    incoming = [
        pl.BlockSpec(
            (senders, per, width), lambda g, p, i=i: (0, i * count + jnp.minimum(g, count - 1), 0)
        )
        for i in range(3)
    ]
    keep_specs = [whole(rows, width), whole(2 * rows, width), whole(2 * rows, width)]
    out_specs = [
        pl.BlockSpec(
            (senders, per, width), lambda g, p: (0, jnp.maximum(g - 1, 0) if leads else g, 0)
        )
    ]
    out_shape = [jax.ShapeDtypeStruct((senders, done * per, width), jnp.bfloat16)]
    if leads:
        out_specs += keep_specs
        out_shape += [
            jax.ShapeDtypeStruct((n * rows, width), jnp.bfloat16) for n in (1, 2, 2)
        ]
    out = pl.pallas_call(
        kernel,
        name="attend" if leads else "attend_rest",
        grid_spec=pltpu.PrefetchScalarGridSpec(
            num_scalar_prefetch=1,
            grid=(steps,),
            in_specs=[whole(nb, rows), *incoming] + ([] if leads else keep_specs),
            out_specs=out_specs,
            scratch_shapes=[
                pltpu.VMEM((total, width), jnp.bfloat16),
                pltpu.VMEM((total, 2 * width), jnp.bfloat16),
                pltpu.VMEM((2, rows, width), jnp.bfloat16),
            ],
        ),
        out_shape=out_shape,
    )(pattern, slots, arrived, arrived, arrived, *(() if leads else kept))
    return out[0], out[1:]


def unpack(order, returned, first, last):
    heads, _, width = returned.shape
    rows = order.shape[2]
    group = 4

    def kernel(order_ref, in_ref, out_ref):
        parts = [
            mm(table_from(order_ref[i], first, last), in_ref[i]).astype(jnp.bfloat16)
            for i in range(group)
        ]
        out_ref[...] = jnp.concatenate(parts, axis=1)

    return pl.pallas_call(
        kernel,
        name="unpack",
        grid=(heads // group,),
        in_specs=[
            pl.BlockSpec((group, 1, rows), lambda h: (h, 0, 0)),
            pl.BlockSpec((group, last - first, width), lambda h: (h, 0, 0)),
        ],
        out_specs=pl.BlockSpec((rows, group * width), lambda h: (0, h)),
        out_shape=jax.ShapeDtypeStruct((rows, heads * width), jnp.bfloat16),
    )(order, returned)


def fetcher(at_ref, arrays, buffer, sems):
    half, cols = arrays[0][0].shape[1:]

    def copy(p, c, source):
        to = buffer.at[p // 2, pl.ds(c * half, half), pl.ds(p % 2 * cols, cols)]
        return pltpu.make_async_copy(source, to, sems.at[p, c])

    def start(slot):
        for p in (2 * slot, 2 * slot + 1):
            for c, kinds in enumerate(arrays):
                for kind, array in enumerate(kinds):

                    @pl.when(at_ref[2 * c, p] == kind)
                    def _():
                        copy(p, c, array.at[at_ref[2 * c + 1, p]]).start()

    def wait(slot):
        for p in (2 * slot, 2 * slot + 1):
            for c, kinds in enumerate(arrays):
                copy(p, c, kinds[0].at[0]).wait()

    return start, wait


def fetch_scratch(count, cells):
    half, cols = cells[0][0].shape[1:]
    return [
        pltpu.VMEM((count // 2, len(cells) * half, 2 * cols), jnp.bfloat16),
        pltpu.SemaphoreType.DMA((count, len(cells))),
    ]


def split(refs, cells):
    kinds = len(cells[0])
    return [refs[c * kinds : (c + 1) * kinds] for c in range(len(cells))], refs[len(cells) * kinds :]


def project(places, attended, cells):
    slots = places.shape[1] // 2
    rows, depth = attended.shape
    wide = 2 * cells[0][0].shape[2]

    def kernel(at_ref, a_ref, *refs):
        arrays, (out_ref, buffer, sems) = split(refs, cells)
        start, wait = fetcher(at_ref, arrays, buffer, sems)
        j = pl.program_id(0)
        for slot in range(slots):

            @pl.when(j == max(slot - 2, 0))
            def _():
                start(slot)

        for slot in range(slots):

            @pl.when(j == slot)
            def _():
                wait(slot)

        out_ref[...] = mm(a_ref[...], buffer[pl.ds(j, 1)][0]).astype(jnp.bfloat16)

    flat = [cell for group in cells for cell in group]
    return pl.pallas_call(
        kernel,
        name="project",
        grid_spec=pltpu.PrefetchScalarGridSpec(
            num_scalar_prefetch=1,
            grid=(slots,),
            in_specs=[pl.BlockSpec((rows, depth), lambda j, at: (0, 0))]
            + [pl.BlockSpec(memory_space=pl.ANY)] * len(flat),
            out_specs=pl.BlockSpec((rows, wide), lambda j, at: (0, j)),
            scratch_shapes=fetch_scratch(2 * slots, cells),
        ),
        out_shape=jax.ShapeDtypeStruct((rows, slots * wide), jnp.bfloat16),
    )(places, attended, *flat)


def unpack_project(order, returned, first, last, partial, places, cells):
    heads, _, width = returned.shape
    rows = order.shape[2]
    slots = places.shape[1] // 2
    wide = 2 * cells[0][0].shape[2]
    group = 4
    turns = heads // group

    def kernel(at_ref, order_ref, in_ref, part_ref, *refs):
        arrays, (out_ref, att_ref, whole, buffer, sems) = split(refs, cells)
        start, wait = fetcher(at_ref, arrays, buffer, sems)
        g = pl.program_id(0)
        for slot in range(slots):

            @pl.when(g == min(slot, turns - 1))
            def _():
                start(slot)

        @pl.when(g < turns)
        def _():
            parts = [
                mm(table_from(order_ref[i], first, last), in_ref[i]).astype(jnp.bfloat16)
                for i in range(group)
            ]
            put = jnp.concatenate(parts, axis=1) + part_ref[...]
            att_ref[...] = put
            whole[pl.ds(g, 1)] = put[None]

        for slot in range(slots):

            @pl.when(g == turns + slot)
            def _():
                wait(slot)
                attended = jnp.concatenate([whole[t] for t in range(turns)], axis=1)
                out_ref[...] = mm(attended, buffer[slot]).astype(jnp.bfloat16)

    flat = [cell for cells_ in cells for cell in cells_]
    turn = lambda g: jnp.minimum(g, turns - 1)
    columns = pl.BlockSpec((rows, group * width), lambda g, at: (0, turn(g)))
    return pl.pallas_call(
        kernel,
        name="unpack_project",
        grid_spec=pltpu.PrefetchScalarGridSpec(
            num_scalar_prefetch=1,
            grid=(turns + slots,),
            in_specs=[
                pl.BlockSpec((group, 1, rows), lambda g, at: (turn(g), 0, 0)),
                pl.BlockSpec((group, last - first, width), lambda g, at: (turn(g), 0, 0)),
                columns,
            ]
            + [pl.BlockSpec(memory_space=pl.ANY)] * len(flat),
            out_specs=[
                pl.BlockSpec((rows, wide), lambda g, at: (0, jnp.maximum(g - turns, 0))),
                columns,
            ],
            scratch_shapes=[pltpu.VMEM((turns, rows, group * width), jnp.bfloat16)]
            + fetch_scratch(2 * slots, cells),
        ),
        out_shape=[
            jax.ShapeDtypeStruct((rows, slots * wide), jnp.bfloat16),
            jax.ShapeDtypeStruct((rows, heads * width), jnp.bfloat16),
        ],
    )(places, order, returned, partial, *flat)


def gather_weights(w_out):
    count = lax.axis_size("seq")
    line = count // 4
    me = lax.axis_index("seq")
    moves = {f"right{n}": [(i, i + 4) for i in range(4 * (n - 1), count - 4)] for n in range(1, line)}
    moves |= {f"left{n}": [(i + 4, i) for i in range(count - 4 * n)] for n in range(1, line)}
    moves |= {
        "x": [(i, i ^ 1) for i in range(count)],
        "y": [(i, i ^ 2) for i in range(count)],
    }

    def moved(cells, way):
        return lax.ppermute(cells, "seq", moves[way])

    half = w_out.shape[0] // 2
    own = (w_out[None, :half], w_out[None, half:])
    from_left, from_right = [w_out], [w_out]
    from_left.append(moved(w_out, "right1"))
    from_right.append(moved(w_out, "left1"))
    ways = (("y", "x"), ("x", "y"))

    def spread(cells):
        both = []
        for color, (inner, outer) in enumerate(ways):
            here = cells[color]
            over_inner = moved(here, inner)
            over_outer = moved(here, outer)
            both.append([here, over_inner, over_outer, moved(over_inner, outer)])
        return both

    near = spread(own)
    for hop in range(2, line):
        from_left.append(moved(from_left[-1], f"right{hop}"))
        from_right.append(moved(from_right[-1], f"left{hop}"))
    middle = from_left[2] + from_right[2]
    middle = [middle[None, :half], middle[None, half:]]
    mid = spread(middle)
    ends = [from_left[1] + from_right[3], from_left[3] + from_right[1]]
    ends = [jnp.stack([cell[at : at + half] for cell in ends]) for at in (0, half)]
    far = spread(ends)
    cells = [[*near[c], *mid[c], *far[c]] for c in range(2)]
    names = jnp.arange(count, dtype=jnp.int32)
    step = jnp.mod(me // 4 - names // 4, line)
    odd = step & 1
    group = jnp.where(step == 0, 0, 1 + odd)
    differ = jnp.bitwise_xor(me, names)
    x_bit, y_bit = differ & 1, (differ >> 1) & 1
    spot = jnp.where(odd == 1, step >> 1, 0)
    places = []
    for inner, outer in ((y_bit, x_bit), (x_bit, y_bit)):
        places += [4 * group + 2 * outer + inner, spot]
    return cells, jnp.stack(places)


def head_shards(queries, keys, values, route, members, pattern, w_out):
    heads, rows = route.shape
    count = lax.axis_size("seq")
    per = rows // count
    entries = pattern.shape[1] * pattern.shape[2]
    early = count // 2 + 1
    cut, cut_back = early * per, (early - 1) * per
    pattern = jnp.pad(pattern.reshape(heads, entries), ((0, 0), (0, LANES - entries)))

    def exchange(cells):
        return lax.all_to_all(cells, "seq", split_axis=0, concat_axis=0, tiled=True)

    cells, place = gather_weights(w_out)
    packed, order = pack(route, pattern, queries, keys, values, 0, cut)
    packed_rest = pack(route, pattern, queries, keys, values, cut, rows, order)
    arrived = exchange(packed)
    arrived_rest = exchange(packed_rest)
    slots, pattern = tail_of(arrived, rows, entries)
    context, kept = attend(slots, pattern, arrived, early)
    returned = exchange(context)
    context_rest, _ = attend(slots, pattern, arrived_rest, count - early, kept)
    returned_rest = exchange(context_rest)
    attended = unpack(order, returned, 0, cut_back)
    mine = lax.axis_index("tp")
    part = count // 2

    def places(which):
        return lax.dynamic_slice_in_dim(place, which * part, part, 1)

    send, attended = unpack_project(
        order, returned_rest, cut_back, rows, attended, places(1 - mine), cells
    )
    received = lax.ppermute(send, "tp", [(0, 1), (1, 0)])
    keep = project(places(mine), attended, cells)
    return (keep.astype(jnp.float32) + received.astype(jnp.float32)).astype(jnp.bfloat16)


def choose(mesh):
    count, groups = mesh.shape["seq"], mesh.shape["tp"]

    def shards(queries, keys, values, route, members, pattern, w_out):
        heads, rows = route.shape
        split = heads == count and groups == 2 and count == 4 * 4
        tiles = rows == REACH * CLUSTER and queries.shape[1] == heads * LANES
        body = head_shards if split and tiles else slot_shards
        return body(queries, keys, values, route, members, pattern, w_out)

    return shards


def solution(mesh):
    placed = (
        P("seq", "tp"),
        P("seq", "tp"),
        P("seq", "tp"),
        P("tp", "seq"),
        P("tp", "seq"),
        P("tp", "seq", None),
        P("tp", "seq"),
    )
    return jax.shard_map(
        choose(mesh), mesh=mesh, in_specs=placed, out_specs=P("seq", "tp"), check_vma=False
    )
```

profile of v0, /device:TPU:0, one launch (start us, length us, event | category | flops | bytes accessed | tf_op | source)
XLA Modules:
  0.0 436.9 jit_solution(4132151800004615604)
XLA Ops:
  1.5 10.4 %pack.1 = (bf16[16,880,128]{2,1,0:T(8,128)(2,1)}, s32[16,1,512]{2,1,0:T(1,128)}) custom-call(s32[16,512]{1,0:T(8,128)} %route_ref.1, s32[16,128]{1,0:T(8,128)} %pad.4.pat_ref, bf16[512,2048]{1,0:T(8,128)(2,1)} %q_ref.3, bf16[512,2048]{1,0:T(8,128)(2,1)} %k_ref.3, bf16[512,2048]{1,0:T(8,128)(2,1)} %v_ref.3), custom_call_target="tpu_custom_call" | custom-call | tf_op jit(solution)/shard_map/pack/pallas_call | solution.py:232
  11.9 8.4 %all-to-all-start = ((bf16[16,880,128]{2,1,0:T(8,128)(2,1)}), bf16[16,880,128]{2,1,0:T(8,128)(2,1)}, u32[]{:S(2)}, u32[]{:S(2)}) async-start(bf16[16,880,128]{2,1,0:T(8,128)(2,1)} %get-tuple-element.14), calls=%async_computation | async-start | bytes 7208960 | tf_op jit(solution)/shard_map/all_to_all | solution.py:615
  20.3 8.0 %pack_rest.1 = bf16[16,672,128]{2,1,0:T(8,128)(2,1)} custom-call(s32[16,1,512]{2,1,0:T(1,128)} %get-tuple-element.13.order_ref, bf16[512,2048]{1,0:T(8,128)(2,1)} %q_ref.3, bf16[512,2048]{1,0:T(8,128)(2,1)} %k_ref.3, bf16[512,2048]{1,0:T(8,128)(2,1)} %v_ref.3), custom_call_target="tpu_custom_call" | custom-call | tf_op jit(solution)/shard_map/pack_rest/pallas_call | solution.py:224
  28.3 60.9 %all-to-all-done.q_ref.k_ref.v_ref = bf16[16,880,128]{2,1,0:T(8,128)(2,1)} async-done(((bf16[16,880,128]{2,1,0:T(8,128)(2,1)}), bf16[16,880,128]{2,1,0:T(8,128)(2,1)}, u32[]{:S(2)}, u32[]{:S(2)}) %all-to-all-start) | async-done | bytes 3604512 | tf_op jit(solution)/shard_map/all_to_all | solution.py:615
  89.2 17.4 %all-to-all-start.1 = ((bf16[16,672,128]{2,1,0:T(8,128)(2,1)}), bf16[16,672,128]{2,1,0:T(8,128)(2,1)S(1)}, u32[]{:S(2)}, u32[]{:S(2)}) async-start(bf16[16,672,128]{2,1,0:T(8,128)(2,1)} %pack_rest.1), calls=%async_computation.1 | async-start | bytes 5505024 | tf_op jit(solution)/shard_map/all_to_all | solution.py:615
  107.9 4.6 %collective-permute-start.3 = (bf16[2048,256]{1,0:T(8,128)(2,1)}, bf16[2048,256]{1,0:T(8,128)(2,1)S(1)}, u32[]{:S(2)}, u32[]{:S(2)}) collective-permute-start(bf16[2048,256]{1,0:T(8,128)(2,1)} %param.12), channel_id=1, source_target_pairs={{0,8},{2,10},{4,12},{6,14},{8,16},{10,18},{12,20},{14,22},{16,24},... | collective-permute-start | bytes 3145736 | tf_op jit(solution)/shard_map/ppermute | solution.py:563
  112.5 62.3 %collective-permute-done.5 = bf16[2048,256]{1,0:T(8,128)(2,1)S(1)} collective-permute-done((bf16[2048,256]{1,0:T(8,128)(2,1)}, bf16[2048,256]{1,0:T(8,128)(2,1)S(1)}, u32[]{:S(2)}, u32[]{:S(2)}) %collective-permute-start.5) | collective-permute-done | bytes 1048608 | tf_op jit(solution)/shard_map/ppermute | solution.py:563
  177.2 1.7 collective-permute-start.4
  178.9 37.7 %collective-permute-done.6 = bf16[2048,256]{1,0:T(8,128)(2,1)} collective-permute-done((bf16[2048,256]{1,0:T(8,128)(2,1)S(1)}, bf16[2048,256]{1,0:T(8,128)(2,1)}, u32[]{:S(2)}, u32[]{:S(2)}) %collective-permute-start.6) | collective-permute-done | bytes 1048608 | tf_op jit(solution)/shard_map/ppermute | solution.py:563
  217.9 1.6 collective-permute-start.11
  222.0 20.7 %attend.1 = (bf16[16,256,128]{2,1,0:T(8,128)(2,1)}, bf16[512,128]{1,0:T(8,128)(2,1)}, bf16[1024,128]{1,0:T(8,128)(2,1)}, bf16[1024,128]{1,0:T(8,128)(2,1)}) custom-call(s32[320]{0:T(512)} %reshape_squeeze.3.pat_ref, s32[16,512]{1,0:T(8,128)} %reshape.140.slot_ref, bf16[16,880,128]{2,1,0:T(8,128)(2,1)} %all-to-all-done.q_ref.k_ref.v_ref, ...), custom_call_target="tpu_custom_call" | custom-call | tf_op jit(solution)/shard_map/attend/pallas_call | solution.py:366
  242.7 9.4 %all-to-all-start.3 = ((bf16[16,256,128]{2,1,0:T(8,128)(2,1)}), bf16[16,256,128]{2,1,0:T(8,128)(2,1)}, u32[]{:S(2)}, u32[]{:S(2)}) async-start(bf16[16,256,128]{2,1,0:T(8,128)(2,1)} %get-tuple-element.18), calls=%async_computation.3 | async-start | bytes 2097152 | tf_op jit(solution)/shard_map/all_to_all | solution.py:615
  253.4 1.9 collective-permute-start.15
  257.4 1.8 add.124
  260.1 18.2 %collective-permute-done.15.refs_13_ = bf16[1,1024,256]{2,1,0:T(8,128)(2,1)} collective-permute-done((bf16[1,1024,256]{2,1,0:T(8,128)(2,1)S(1)}, bf16[1,1024,256]{2,1,0:T(8,128)(2,1)}, u32[]{:S(2)}, u32[]{:S(2)}) %collective-permute-start.15) | collective-permute-done | bytes 524320 | tf_op jit(solution)/shard_map/ppermute | solution.py:563
  282.0 2.0 collective-permute-start.18
  285.9 3.5 collective-permute-done.1.refs_2_
  290.9 2.2 collective-permute-done.16.refs_14_
  293.9 19.5 %attend_rest.1 = bf16[16,256,128]{2,1,0:T(8,128)(2,1)} custom-call(s32[320]{0:T(512)} %reshape_squeeze.3.pat_ref, s32[16,512]{1,0:T(8,128)} %reshape.140.slot_ref, bf16[16,672,128]{2,1,0:T(8,128)(2,1)} %copy-done, bf16[16,672,128]{2,1,0:T(8,128)(2,1)} %copy-done, bf16[16,672,128]{2,1,0:T(8,128)(2,1)} %copy-done, bf16[512,128]{1,0:T(8,128)(2,1)} %get-tuple-element.15.refs_0_, ...), custom_call_target="tpu_custom_call" | custom-call | tf_op jit(solution)/shard_map/attend_rest/pallas_call | solution.py:366
  313.4 5.5 %all-to-all-start.2 = ((bf16[16,256,128]{2,1,0:T(8,128)(2,1)}), bf16[16,256,128]{2,1,0:T(8,128)(2,1)}, u32[]{:S(2)}, u32[]{:S(2)}) async-start(bf16[16,256,128]{2,1,0:T(8,128)(2,1)} %attend_rest.1), calls=%async_computation.2 | async-start | bytes 2097152 | tf_op jit(solution)/shard_map/all_to_all | solution.py:615
  318.9 1.9 collective-permute-start.7
  321.0 1.9 collective-permute-start.8
  322.9 25.8 %collective-permute-done.7.refs_5_ = bf16[1,1024,256]{2,1,0:T(8,128)(2,1)} collective-permute-done((bf16[1,1024,256]{2,1,0:T(8,128)(2,1)S(1)}, bf16[1,1024,256]{2,1,0:T(8,128)(2,1)}, u32[]{:S(2)}, u32[]{:S(2)}) %collective-permute-start.7) | collective-permute-done | bytes 524320 | tf_op jit(solution)/shard_map/ppermute | solution.py:563
  348.7 2.1 collective-permute-start.20
  350.8 9.0 %collective-permute-done.19.refs_18_ = bf16[1,1024,256]{2,1,0:T(8,128)(2,1)S(1)} collective-permute-done((bf16[1,1024,256]{2,1,0:T(8,128)(2,1)S(1)}, bf16[1,1024,256]{2,1,0:T(8,128)(2,1)S(1)}, u32[]{:S(2)}, u32[]{:S(2)}) %collective-permute-start.19) | collective-permute-done | bytes 524320 | tf_op jit(solution)/shard_map/ppermute | solution.py:563
  360.6 2.0 collective-permute-start.22
  364.1 6.9 %collective-permute-done.20.refs_19_ = bf16[1,1024,256]{2,1,0:T(8,128)(2,1)S(1)} collective-permute-done((bf16[1,1024,256]{2,1,0:T(8,128)(2,1)}, bf16[1,1024,256]{2,1,0:T(8,128)(2,1)S(1)}, u32[]{:S(2)}, u32[]{:S(2)}) %collective-permute-start.20) | collective-permute-done | bytes 524320 | tf_op jit(solution)/shard_map/ppermute | solution.py:563
  373.3 4.5 %unpack.1.part_ref = bf16[512,2048]{1,0:T(8,128)(2,1)} custom-call(s32[16,1,512]{2,1,0:T(1,128)} %get-tuple-element.13.order_ref, bf16[16,256,128]{2,1,0:T(8,128)(2,1)} %all-to-all-done.3.in_ref), custom_call_target="tpu_custom_call" | custom-call | tf_op jit(solution)/shard_map/unpack/pallas_call | solution.py:397
  377.8 32.0 %collective-permute-done.9.refs_7_ = bf16[1,1024,256]{2,1,0:T(8,128)(2,1)} collective-permute-done((bf16[1,1024,256]{2,1,0:T(8,128)(2,1)}, bf16[1,1024,256]{2,1,0:T(8,128)(2,1)}, u32[]{:S(2)}, u32[]{:S(2)}) %collective-permute-start.9) | collective-permute-done | bytes 524320 | tf_op jit(solution)/shard_map/ppermute | solution.py:563
  410.9 12.2 %unpack_project.1 = (bf16[512,2048]{1,0:T(8,128)(2,1)}, bf16[512,2048]{1,0:T(8,128)(2,1)}) custom-call(s32[4,8]{1,0:T(4,128)} %get-tuple-element.30.at_ref, s32[16,1,512]{2,1,0:T(1,128)} %get-tuple-element.13.order_ref, bf16[16,256,128]{2,1,0:T(8,128)(2,1)} %all-to-all-done.2.in_ref, bf16[512,2048]{1,0:T(8,128)(2,1)} %unpack.1.part_ref, ...), custom_call_target="tpu_custom_call" | custom-call | tf_op jit(solution)/shard_map/unpack_project/pallas_call | solution.py:525
  423.2 10.0 %project.1 = bf16[512,2048]{1,0:T(8,128)(2,1)} custom-call(s32[4,8]{1,0:T(4,128)} %get-tuple-element.29.at_ref, bf16[512,2048]{1,0:T(8,128)(2,1)} %get-tuple-element.19.a_ref, bf16[1,1024,256]{2,1,0:T(8,128)(2,1)} %copy-done.4, bf16[1,1024,256]{2,1,0:T(8,128)(2,1)} %collective-permute-done.refs_1_, bf16[1,1024,256]{2,1,0:T(8,128)(2,1)} %copy-done.8, ...), custom_call_target="tpu_custom_call" | custom-call | tf_op jit(solution)/shard_map/project/pallas_call | solution.py:471
  433.2 3.7 add_convert_fusion
  (91 shorter events, 26.5 us)
Async XLA Ops:
  11.9 77.3 %all-to-all-start = ((bf16[16,880,128]{2,1,0:T(8,128)(2,1)}), bf16[16,880,128]{2,1,0:T(8,128)(2,1)}, u32[]{:S(2)}, u32[]{:S(2)}) async-start(bf16[16,880,128]{2,1,0:T(8,128)(2,1)} %get-tuple-element.14), calls=%async_computation | async-start | bytes 7208960 | tf_op jit(solution)/shard_map/all_to_all | solution.py:615
  89.2 153.5 %all-to-all-start.1 = ((bf16[16,672,128]{2,1,0:T(8,128)(2,1)}), bf16[16,672,128]{2,1,0:T(8,128)(2,1)S(1)}, u32[]{:S(2)}, u32[]{:S(2)}) async-start(bf16[16,672,128]{2,1,0:T(8,128)(2,1)} %pack_rest.1), calls=%async_computation.1 | async-start | bytes 5505024 | tf_op jit(solution)/shard_map/all_to_all | solution.py:615
  106.6 68.2 %collective-permute-start.5 = (bf16[2048,256]{1,0:T(8,128)(2,1)}, bf16[2048,256]{1,0:T(8,128)(2,1)S(1)}, u32[]{:S(2)}, u32[]{:S(2)}) collective-permute-start(bf16[2048,256]{1,0:T(8,128)(2,1)} %param.12), channel_id=1, source_target_pairs={{8,0},{10,2},{12,4},{14,6},{16,8},{18,10},{20,12},{22,14},{24,16},... | collective-permute-start | bytes 3145736 | tf_op jit(solution)/shard_map/ppermute | solution.py:563
  107.9 69.2 %collective-permute-start.3 = (bf16[2048,256]{1,0:T(8,128)(2,1)}, bf16[2048,256]{1,0:T(8,128)(2,1)S(1)}, u32[]{:S(2)}, u32[]{:S(2)}) collective-permute-start(bf16[2048,256]{1,0:T(8,128)(2,1)} %param.12), channel_id=1, source_target_pairs={{0,8},{2,10},{4,12},{6,14},{8,16},{10,18},{12,20},{14,22},{16,24},... | collective-permute-start | bytes 3145736 | tf_op jit(solution)/shard_map/ppermute | solution.py:563
  175.8 40.8 %collective-permute-start.6 = (bf16[2048,256]{1,0:T(8,128)(2,1)S(1)}, bf16[2048,256]{1,0:T(8,128)(2,1)}, u32[]{:S(2)}, u32[]{:S(2)}) collective-permute-start(bf16[2048,256]{1,0:T(8,128)(2,1)S(1)} %collective-permute-done.5), channel_id=1, source_target_pairs={{8,0},{10,2},{12,4},{14,6},{16,8},{18,10},{20,12},{22,14},{9,1},{1... | collective-permute-start | bytes 3145736 | tf_op jit(solution)/shard_map/ppermute | solution.py:563
  177.2 40.8 %collective-permute-start.4 = (bf16[2048,256]{1,0:T(8,128)(2,1)S(1)}, bf16[2048,256]{1,0:T(8,128)(2,1)}, u32[]{:S(2)}, u32[]{:S(2)}) collective-permute-start(bf16[2048,256]{1,0:T(8,128)(2,1)S(1)} %collective-permute-done.3), channel_id=1, source_target_pairs={{8,16},{10,18},{12,20},{14,22},{16,24},{18,26},{20,28},{22,30},{9,... | collective-permute-start | bytes 3145736 | tf_op jit(solution)/shard_map/ppermute | solution.py:563
  216.6 63.7 %collective-permute-start.10 = (bf16[2048,256]{1,0:T(8,128)(2,1)}, bf16[2048,256]{1,0:T(8,128)(2,1)}, u32[]{:S(2)}, u32[]{:S(2)}) collective-permute-start(bf16[2048,256]{1,0:T(8,128)(2,1)} %collective-permute-done.6), channel_id=1, source_target_pairs={{8,0},{10,2},{12,4},{14,6},{9,1},{11,3},{13,5},{15,7}} | collective-permute-start | bytes 3145736 | tf_op jit(solution)/shard_map/ppermute | solution.py:563
  217.9 64.0 %collective-permute-start.11 = (bf16[2048,256]{1,0:T(8,128)(2,1)}, bf16[2048,256]{1,0:T(8,128)(2,1)}, u32[]{:S(2)}, u32[]{:S(2)}) collective-permute-start(bf16[2048,256]{1,0:T(8,128)(2,1)} %collective-permute-done.4), channel_id=1, source_target_pairs={{16,24},{18,26},{20,28},{22,30},{17,25},{19,27},{21,29},{23,31}} | collective-permute-start | bytes 3145736 | tf_op jit(solution)/shard_map/ppermute | solution.py:563
  242.7 70.7 %all-to-all-start.3 = ((bf16[16,256,128]{2,1,0:T(8,128)(2,1)}), bf16[16,256,128]{2,1,0:T(8,128)(2,1)}, u32[]{:S(2)}, u32[]{:S(2)}) async-start(bf16[16,256,128]{2,1,0:T(8,128)(2,1)} %get-tuple-element.18), calls=%async_computation.3 | async-start | bytes 2097152 | tf_op jit(solution)/shard_map/all_to_all | solution.py:615
  253.4 24.9 %collective-permute-start.15 = (bf16[1,1024,256]{2,1,0:T(8,128)(2,1)S(1)}, bf16[1,1024,256]{2,1,0:T(8,128)(2,1)}, u32[]{:S(2)}, u32[]{:S(2)}) collective-permute-start(bf16[1,1024,256]{2,1,0:T(8,128)(2,1)S(1)} %get-tuple-element.27.refs_12_), channel_id=1, source_target_pairs={{0,2},{2,0},{4,6},{6,4},{8,10},{10,8},{12,14},{14,12},{16,18},{18,... | collective-permute-start | bytes 1572872 | tf_op jit(solution)/shard_map/ppermute | solution.py:563
  255.4 24.4 %collective-permute-start = (bf16[1,1024,256]{2,1,0:T(8,128)(2,1)S(1)}, bf16[1,1024,256]{2,1,0:T(8,128)(2,1)}, u32[]{:S(2)}, u32[]{:S(2)}) collective-permute-start(bf16[1,1024,256]{2,1,0:T(8,128)(2,1)S(1)} %get-tuple-element.28.refs_0_), channel_id=1, source_target_pairs={{0,4},{2,6},{4,0},{6,2},{8,12},{10,14},{12,8},{14,10},{16,20},{18,... | collective-permute-start | bytes 1572872 | tf_op jit(solution)/shard_map/ppermute | solution.py:563
  256.8 32.6 %collective-permute-start.1 = (bf16[1,1024,256]{2,1,0:T(8,128)(2,1)S(1)}, bf16[1,1024,256]{2,1,0:T(8,128)(2,1)S(1)}, u32[]{:S(2)}, u32[]{:S(2)}) collective-permute-start(bf16[1,1024,256]{2,1,0:T(8,128)(2,1)S(1)} %get-tuple-element.28.refs_0_), channel_id=1, source_target_pairs={{0,2},{2,0},{4,6},{6,4},{8,10},{10,8},{12,14},{14,12},{16,18},{18,... | collective-permute-start | bytes 1572872 | tf_op jit(solution)/shard_map/ppermute | solution.py:563
  260.1 60.8 %copy-start.5 = (bf16[1,1024,256]{2,1,0:T(8,128)(2,1)}, bf16[1,1024,256]{2,1,0:T(8,128)(2,1)S(1)}, u32[]{:S(2)}) copy-start(bf16[1,1024,256]{2,1,0:T(8,128)(2,1)S(1)} %get-tuple-element.25.refs_16_) | copy-start | bytes 1572868
  278.3 14.8 %collective-permute-start.16 = (bf16[1,1024,256]{2,1,0:T(8,128)(2,1)S(1)}, bf16[1,1024,256]{2,1,0:T(8,128)(2,1)S(1)}, u32[]{:S(2)}, u32[]{:S(2)}) collective-permute-start(bf16[1,1024,256]{2,1,0:T(8,128)(2,1)S(1)} %get-tuple-element.27.refs_12_), channel_id=1, source_target_pairs={{0,4},{2,6},{4,0},{6,2},{8,12},{10,14},{12,8},{14,10},{16,20},{18,... | collective-permute-start | bytes 1572872 | tf_op jit(solution)/shard_map/ppermute | solution.py:563
  279.8 39.1 %collective-permute-start.17 = (bf16[1,1024,256]{2,1,0:T(8,128)(2,1)}, bf16[1,1024,256]{2,1,0:T(8,128)(2,1)}, u32[]{:S(2)}, u32[]{:S(2)}) collective-permute-start(bf16[1,1024,256]{2,1,0:T(8,128)(2,1)} %collective-permute-done.15.refs_13_), channel_id=1, source_target_pairs={{0,4},{2,6},{4,0},{6,2},{8,12},{10,14},{12,8},{14,10},{16,20},{18,... | collective-permute-start | bytes 1572872 | tf_op jit(solution)/shard_map/ppermute | solution.py:563
  280.3 40.5 %collective-permute-start.2 = (bf16[1,1024,256]{2,1,0:T(8,128)(2,1)}, bf16[1,1024,256]{2,1,0:T(8,128)(2,1)}, u32[]{:S(2)}, u32[]{:S(2)}) collective-permute-start(bf16[1,1024,256]{2,1,0:T(8,128)(2,1)} %collective-permute-done.refs_1_), channel_id=1, source_target_pairs={{0,2},{2,0},{4,6},{6,4},{8,10},{10,8},{12,14},{14,12},{16,18},{18,... | collective-permute-start | bytes 1572872 | tf_op jit(solution)/shard_map/ppermute | solution.py:563
  282.0 39.1 %collective-permute-start.18 = (bf16[1,1024,256]{2,1,0:T(8,128)(2,1)S(1)}, bf16[1,1024,256]{2,1,0:T(8,128)(2,1)}, u32[]{:S(2)}, u32[]{:S(2)}) collective-permute-start(bf16[1,1024,256]{2,1,0:T(8,128)(2,1)S(1)} %get-tuple-element.25.refs_16_), channel_id=1, source_target_pairs={{0,2},{2,0},{4,6},{6,4},{8,10},{10,8},{12,14},{14,12},{16,18},{18,... | collective-permute-start | bytes 1572872 | tf_op jit(solution)/shard_map/ppermute | solution.py:563
  285.8 74.0 %copy-start.1 = (bf16[2,1024,256]{2,1,0:T(8,128)(2,1)}, bf16[2,1024,256]{2,1,0:T(8,128)(2,1)S(1)}, u32[]{:S(2)}) copy-start(bf16[2,1024,256]{2,1,0:T(8,128)(2,1)S(1)} %pad_maximum_fusion.refs_8_) | copy-start | bytes 3145732
  285.9 74.7 %copy-start.2 = (bf16[2,1024,256]{2,1,0:T(8,128)(2,1)}, bf16[2,1024,256]{2,1,0:T(8,128)(2,1)S(1)}, u32[]{:S(2)}) copy-start(bf16[2,1024,256]{2,1,0:T(8,128)(2,1)S(1)} %pad_maximum_fusion.1.refs_20_) | copy-start | bytes 3145732
  289.4 73.2 %collective-permute-start.12 = (bf16[2,1024,256]{2,1,0:T(8,128)(2,1)S(1)}, bf16[2,1024,256]{2,1,0:T(8,128)(2,1)}, u32[]{:S(2)}, u32[]{:S(2)}) collective-permute-start(bf16[2,1024,256]{2,1,0:T(8,128)(2,1)S(1)} %pad_maximum_fusion.refs_8_), channel_id=1, source_target_pairs={{0,4},{2,6},{4,0},{6,2},{8,12},{10,14},{12,8},{14,10},{16,20},{18,... | collective-permute-start | bytes 3145736 | tf_op jit(solution)/shard_map/ppermute | solution.py:563
  293.1 70.9 %collective-permute-start.21 = (bf16[2,1024,256]{2,1,0:T(8,128)(2,1)S(1)}, bf16[2,1024,256]{2,1,0:T(8,128)(2,1)}, u32[]{:S(2)}, u32[]{:S(2)}) collective-permute-start(bf16[2,1024,256]{2,1,0:T(8,128)(2,1)S(1)} %pad_maximum_fusion.1.refs_20_), channel_id=1, source_target_pairs={{0,2},{2,0},{4,6},{6,4},{8,10},{10,8},{12,14},{14,12},{16,18},{18,... | collective-permute-start | bytes 3145736 | tf_op jit(solution)/shard_map/ppermute | solution.py:563
  313.4 96.6 %all-to-all-start.2 = ((bf16[16,256,128]{2,1,0:T(8,128)(2,1)}), bf16[16,256,128]{2,1,0:T(8,128)(2,1)}, u32[]{:S(2)}, u32[]{:S(2)}) async-start(bf16[16,256,128]{2,1,0:T(8,128)(2,1)} %attend_rest.1), calls=%async_computation.2 | async-start | bytes 2097152 | tf_op jit(solution)/shard_map/all_to_all | solution.py:615
  318.9 29.8 %collective-permute-start.7 = (bf16[1,1024,256]{2,1,0:T(8,128)(2,1)S(1)}, bf16[1,1024,256]{2,1,0:T(8,128)(2,1)}, u32[]{:S(2)}, u32[]{:S(2)}) collective-permute-start(bf16[1,1024,256]{2,1,0:T(8,128)(2,1)S(1)} %copy-done.6), channel_id=1, source_target_pairs={{0,4},{2,6},{4,0},{6,2},{8,12},{10,14},{12,8},{14,10},{16,20},{18,... | collective-permute-start | bytes 1572872 | tf_op jit(solution)/shard_map/ppermute | solution.py:563
  320.9 39.0 %collective-permute-start.19 = (bf16[1,1024,256]{2,1,0:T(8,128)(2,1)S(1)}, bf16[1,1024,256]{2,1,0:T(8,128)(2,1)S(1)}, u32[]{:S(2)}, u32[]{:S(2)}) collective-permute-start(bf16[1,1024,256]{2,1,0:T(8,128)(2,1)S(1)} %get-tuple-element.25.refs_16_), channel_id=1, source_target_pairs={{0,4},{2,6},{4,0},{6,2},{8,12},{10,14},{12,8},{14,10},{16,20},{18,... | collective-permute-start | bytes 1572872 | tf_op jit(solution)/shard_map/ppermute | solution.py:563
  321.0 39.5 %collective-permute-start.8 = (bf16[1,1024,256]{2,1,0:T(8,128)(2,1)S(1)}, bf16[1,1024,256]{2,1,0:T(8,128)(2,1)S(1)}, u32[]{:S(2)}, u32[]{:S(2)}) collective-permute-start(bf16[1,1024,256]{2,1,0:T(8,128)(2,1)S(1)} %copy-done.6), channel_id=1, source_target_pairs={{0,2},{2,0},{4,6},{6,4},{8,10},{10,8},{12,14},{14,12},{16,18},{18,... | collective-permute-start | bytes 1572872 | tf_op jit(solution)/shard_map/ppermute | solution.py:563
  348.7 22.4 %collective-permute-start.20 = (bf16[1,1024,256]{2,1,0:T(8,128)(2,1)}, bf16[1,1024,256]{2,1,0:T(8,128)(2,1)S(1)}, u32[]{:S(2)}, u32[]{:S(2)}) collective-permute-start(bf16[1,1024,256]{2,1,0:T(8,128)(2,1)} %collective-permute-done.18.refs_17_), channel_id=1, source_target_pairs={{0,4},{2,6},{4,0},{6,2},{8,12},{10,14},{12,8},{14,10},{16,20},{18,... | collective-permute-start | bytes 1572872 | tf_op jit(solution)/shard_map/ppermute | solution.py:563
  359.8 50.0 %collective-permute-start.13 = (bf16[2,1024,256]{2,1,0:T(8,128)(2,1)S(1)}, bf16[2,1024,256]{2,1,0:T(8,128)(2,1)}, u32[]{:S(2)}, u32[]{:S(2)}) collective-permute-start(bf16[2,1024,256]{2,1,0:T(8,128)(2,1)S(1)} %pad_maximum_fusion.refs_8_), channel_id=1, source_target_pairs={{0,2},{2,0},{4,6},{6,4},{8,10},{10,8},{12,14},{14,12},{16,18},{18,... | collective-permute-start | bytes 3145736 | tf_op jit(solution)/shard_map/ppermute | solution.py:563
  360.6 49.3 %collective-permute-start.22 = (bf16[2,1024,256]{2,1,0:T(8,128)(2,1)S(1)}, bf16[2,1024,256]{2,1,0:T(8,128)(2,1)S(1)}, u32[]{:S(2)}, u32[]{:S(2)}) collective-permute-start(bf16[2,1024,256]{2,1,0:T(8,128)(2,1)S(1)} %pad_maximum_fusion.1.refs_20_), channel_id=1, source_target_pairs={{0,4},{2,6},{4,0},{6,2},{8,12},{10,14},{12,8},{14,10},{16,20},{18,... | collective-permute-start | bytes 3145736 | tf_op jit(solution)/shard_map/ppermute | solution.py:563
  362.6 47.3 %collective-permute-start.14 = (bf16[2,1024,256]{2,1,0:T(8,128)(2,1)}, bf16[2,1024,256]{2,1,0:T(8,128)(2,1)}, u32[]{:S(2)}, u32[]{:S(2)}) collective-permute-start(bf16[2,1024,256]{2,1,0:T(8,128)(2,1)} %collective-permute-done.12.refs_9_), channel_id=1, source_target_pairs={{0,2},{2,0},{4,6},{6,4},{8,10},{10,8},{12,14},{14,12},{16,18},{18,... | collective-permute-start | bytes 3145736 | tf_op jit(solution)/shard_map/ppermute | solution.py:563
  364.1 46.0 %collective-permute-start.23 = (bf16[2,1024,256]{2,1,0:T(8,128)(2,1)}, bf16[2,1024,256]{2,1,0:T(8,128)(2,1)}, u32[]{:S(2)}, u32[]{:S(2)}) collective-permute-start(bf16[2,1024,256]{2,1,0:T(8,128)(2,1)} %collective-permute-done.21.refs_21_), channel_id=1, source_target_pairs={{0,4},{2,6},{4,0},{6,2},{8,12},{10,14},{12,8},{14,10},{16,20},{18,... | collective-permute-start | bytes 3145736 | tf_op jit(solution)/shard_map/ppermute | solution.py:563
  371.9 38.0 %collective-permute-start.9 = (bf16[1,1024,256]{2,1,0:T(8,128)(2,1)}, bf16[1,1024,256]{2,1,0:T(8,128)(2,1)}, u32[]{:S(2)}, u32[]{:S(2)}) collective-permute-start(bf16[1,1024,256]{2,1,0:T(8,128)(2,1)} %collective-permute-done.7.refs_5_), channel_id=1, source_target_pairs={{0,2},{2,0},{4,6},{6,4},{8,10},{10,8},{12,14},{14,12},{16,18},{18,... | collective-permute-start | bytes 1572872 | tf_op jit(solution)/shard_map/ppermute | solution.py:563
  423.1 10.1 %collective-permute-start.24 = (bf16[512,2048]{1,0:T(8,128)(2,1)}, bf16[512,2048]{1,0:T(8,128)(2,1)S(1)}, u32[]{:S(2)}, u32[]{:S(2)}) collective-permute-start(bf16[512,2048]{1,0:T(8,128)(2,1)} %get-tuple-element.20), channel_id=1, source_target_pairs={{0,1},{1,0},{2,3},{3,2},{4,5},{5,4},{6,7},{7,6},{8,9},{9,8},{10,11... | collective-permute-start | bytes 6291464 | tf_op jit(solution)/shard_map/ppermute | solution.py:637
  (14 other events, 151.3 us)
where the time goes:
time: 438 us; the launch traced here: 437 us
  waiting for transfers between devices  259 us (59%)
  Pallas kernels  85.3 us (19%)
  starting transfers between devices  73.3 us (17%)
  other arithmetic  9.69 us (2%)
  local copies, waits for them, and re-layouts  9.32 us (2%)
    ppermute x24, waiting for transfers between devices, moved(): return lax.ppermute(cells, 'seq', moves[way])  198 us
    all_to_all x4, waiting for transfers between devices, exchange(): return lax.all_to_all(cells, 'seq', split_axis=0, concat_axis=0, tiled=True)  60.9 us
    all_to_all x4, starting transfers between devices, exchange(): return lax.all_to_all(cells, 'seq', split_axis=0, concat_axis=0, tiled=True)  40.7 us
    pallas_call x2, Pallas kernels, attend(): pl.pallas_call(kernel, name='attend' if leads else 'attend_rest', grid_sp...  40.2 us
    ppermute x24, starting transfers between devices, moved(): return lax.ppermute(cells, 'seq', moves[way])  32.5 us
    pallas_call x1, Pallas kernels, unpack_project(): pl.pallas_call(kernel, name='unpack_project', grid_spec=pltpu.PrefetchSca...  12.2 us
    pallas_call x1, Pallas kernels, pack(): pl.pallas_call(lead, name='pack', grid=(heads // group,), in_specs=[pl.Bl...  10.4 us
    pallas_call x1, Pallas kernels, project(): pl.pallas_call(kernel, name='project', grid_spec=pltpu.PrefetchScalarGrid...  9.99 us
  transfers between devices with their start and end apart: 29, of which 11 were waited for; matrix products, arithmetic and copies ran while one was open for 2% of the time, Pallas kernels for 14%

commit v1 on v0

--- a/solution.py
+++ b/solution.py
@@ -465,7 +465,8 @@
             def _():
                 wait(slot)
 
-        out_ref[...] = mm(a_ref[...], buffer[pl.ds(j, 1)][0]).astype(jnp.bfloat16)
+        at = pl.ds(pl.multiple_of(j * wide, wide), wide)
+        out_ref[:, at] = mm(a_ref[...], buffer[pl.ds(j, 1)][0]).astype(jnp.bfloat16)
 
     flat = [cell for group in cells for cell in group]
     return pl.pallas_call(
@@ -476,10 +477,10 @@
             grid=(slots,),
             in_specs=[pl.BlockSpec((rows, depth), lambda j, at: (0, 0))]
             + [pl.BlockSpec(memory_space=pl.ANY)] * len(flat),
-            out_specs=pl.BlockSpec((rows, wide), lambda j, at: (0, j)),
+            out_specs=pl.BlockSpec(memory_space=pltpu.VMEM),
             scratch_shapes=fetch_scratch(2 * slots, cells),
         ),
-        out_shape=jax.ShapeDtypeStruct((rows, slots * wide), jnp.bfloat16),
+        out_shape=pltpu.VMEM((rows, slots * wide), jnp.bfloat16),
     )(places, attended, *flat)
 
 
@@ -607,7 +608,7 @@
     count = lax.axis_size("seq")
     per = rows // count
     entries = pattern.shape[1] * pattern.shape[2]
-    early = count // 2 + 1
+    early = count // 2 + 2
     cut, cut_back = early * per, (early - 1) * per
     pattern = jnp.pad(pattern.reshape(heads, entries), ((0, 0), (0, LANES - entries)))
 

time: 438 us -> 444 us (1.014)
    all_to_all x4, waiting for transfers between devices: 60.9 us -> 68.3 us  [exchange(): return lax.all_to_all(cells, 'seq', split_axis=0, concat_axis=0, tiled=True)]
  transfers between devices with their start and end apart: 29 -> 29, of which waited for: 11 -> 11; matrix products, arithmetic and copies ran while one was open for 2% -> 3% of each run, Pallas kernels for 14% -> 14%
where the time goes in v1:
time: 444 us; the launch traced here: 442 us
  waiting for transfers between devices  263 us (59%)
  Pallas kernels  85 us (19%)
  starting transfers between devices  73.8 us (17%)
  other arithmetic  10.3 us (2%)
  local copies, waits for them, and re-layouts  9.72 us (2%)
    ppermute x24, waiting for transfers between devices, moved(): return lax.ppermute(cells, 'seq', moves[way])  195 us
    all_to_all x4, waiting for transfers between devices, exchange(): return lax.all_to_all(cells, 'seq', split_axis=0, concat_axis=0, tiled=True)  68.3 us
    all_to_all x4, starting transfers between devices, exchange(): return lax.all_to_all(cells, 'seq', split_axis=0, concat_axis=0, tiled=True)  42.8 us
    pallas_call x2, Pallas kernels, attend(): pl.pallas_call(kernel, name='attend' if leads else 'attend_rest', grid_sp...  40.2 us
    ppermute x24, starting transfers between devices, moved(): return lax.ppermute(cells, 'seq', moves[way])  31 us
    pallas_call x1, Pallas kernels, unpack_project(): pl.pallas_call(kernel, name='unpack_project', grid_spec=pltpu.PrefetchSca...  12.2 us
    pallas_call x1, Pallas kernels, pack(): pl.pallas_call(lead, name='pack', grid=(heads // group,), in_specs=[pl.Bl...  10.6 us
    pallas_call x1, Pallas kernels, project(): pl.pallas_call(kernel, name='project', grid_spec=pltpu.PrefetchScalarGrid...  9.16 us
  transfers between devices with their start and end apart: 29, of which 11 were waited for; matrix products, arithmetic and copies ran while one was open for 3% of the time, Pallas kernels for 14%

profile of v1, /device:TPU:0, one launch (start us, length us, event | category | flops | bytes accessed | tf_op | source)
XLA Modules:
  0.0 442.3 jit_solution(18082076701031006342)
XLA Ops:
  1.5 10.6 %pack.1 = (bf16[16,976,128]{2,1,0:T(8,128)(2,1)}, s32[16,1,512]{2,1,0:T(1,128)}) custom-call(s32[16,512]{1,0:T(8,128)} %route_ref.1, s32[16,128]{1,0:T(8,128)} %pad.4.pat_ref, bf16[512,2048]{1,0:T(8,128)(2,1)} %q_ref.3, bf16[512,2048]{1,0:T(8,128)(2,1)} %k_ref.3, bf16[512,2048]{1,0:T(8,128)(2,1)} %v_ref.3), custom_call_target="tpu_custom_call" | custom-call | tf_op jit(solution)/shard_map/pack/pallas_call | solution.py:232
  12.1 8.4 %all-to-all-start = ((bf16[16,976,128]{2,1,0:T(8,128)(2,1)}), bf16[16,976,128]{2,1,0:T(8,128)(2,1)}, u32[]{:S(2)}, u32[]{:S(2)}) async-start(bf16[16,976,128]{2,1,0:T(8,128)(2,1)} %get-tuple-element.14), calls=%async_computation | async-start | bytes 7995392 | tf_op jit(solution)/shard_map/all_to_all | solution.py:616
  20.5 7.8 %pack_rest.1 = bf16[16,576,128]{2,1,0:T(8,128)(2,1)} custom-call(s32[16,1,512]{2,1,0:T(1,128)} %get-tuple-element.13.order_ref, bf16[512,2048]{1,0:T(8,128)(2,1)} %q_ref.3, bf16[512,2048]{1,0:T(8,128)(2,1)} %k_ref.3, bf16[512,2048]{1,0:T(8,128)(2,1)} %v_ref.3), custom_call_target="tpu_custom_call" | custom-call | tf_op jit(solution)/shard_map/pack_rest/pallas_call | solution.py:224
  28.3 68.3 %all-to-all-done.q_ref.k_ref.v_ref = bf16[16,976,128]{2,1,0:T(8,128)(2,1)} async-done(((bf16[16,976,128]{2,1,0:T(8,128)(2,1)}), bf16[16,976,128]{2,1,0:T(8,128)(2,1)}, u32[]{:S(2)}, u32[]{:S(2)}) %all-to-all-start) | async-done | bytes 3997728 | tf_op jit(solution)/shard_map/all_to_all | solution.py:616
  96.6 19.3 %all-to-all-start.1 = ((bf16[16,576,128]{2,1,0:T(8,128)(2,1)}), bf16[16,576,128]{2,1,0:T(8,128)(2,1)S(1)}, u32[]{:S(2)}, u32[]{:S(2)}) async-start(bf16[16,576,128]{2,1,0:T(8,128)(2,1)} %pack_rest.1), calls=%async_computation.1 | async-start | bytes 4718592 | tf_op jit(solution)/shard_map/all_to_all | solution.py:616
  117.2 4.6 %collective-permute-start.3 = (bf16[2048,256]{1,0:T(8,128)(2,1)S(1)}, bf16[2048,256]{1,0:T(8,128)(2,1)S(1)}, u32[]{:S(2)}, u32[]{:S(2)}) collective-permute-start(bf16[2048,256]{1,0:T(8,128)(2,1)S(1)} %copy-done.17), channel_id=1, source_target_pairs={{0,8},{2,10},{4,12},{6,14},{8,16},{10,18},{12,20},{14,22},{16,24},... | collective-permute-start | bytes 3145736 | tf_op jit(solution)/shard_map/ppermute | solution.py:564
  121.8 56.0 %collective-permute-done.5 = bf16[2048,256]{1,0:T(8,128)(2,1)S(1)} collective-permute-done((bf16[2048,256]{1,0:T(8,128)(2,1)S(1)}, bf16[2048,256]{1,0:T(8,128)(2,1)S(1)}, u32[]{:S(2)}, u32[]{:S(2)}) %collective-permute-start.5) | collective-permute-done | bytes 1048608 | tf_op jit(solution)/shard_map/ppermute | solution.py:564
  180.1 1.6 collective-permute-start.4
  181.8 35.7 %collective-permute-done.6 = bf16[2048,256]{1,0:T(8,128)(2,1)} collective-permute-done((bf16[2048,256]{1,0:T(8,128)(2,1)S(1)}, bf16[2048,256]{1,0:T(8,128)(2,1)}, u32[]{:S(2)}, u32[]{:S(2)}) %collective-permute-start.6) | collective-permute-done | bytes 1048608 | tf_op jit(solution)/shard_map/ppermute | solution.py:564
  218.8 1.7 collective-permute-start.11
  223.5 1.6 reshape.140.slot_ref
  225.8 22.9 %attend.1 = (bf16[16,288,128]{2,1,0:T(8,128)(2,1)}, bf16[512,128]{1,0:T(8,128)(2,1)}, bf16[1024,128]{1,0:T(8,128)(2,1)}, bf16[1024,128]{1,0:T(8,128)(2,1)}) custom-call(s32[320]{0:T(512)} %reshape_squeeze.3.pat_ref, s32[16,512]{1,0:T(8,128)} %reshape.140.slot_ref, bf16[16,976,128]{2,1,0:T(8,128)(2,1)} %all-to-all-done.q_ref.k_ref.v_ref, ...), custom_call_target="tpu_custom_call" | custom-call | tf_op jit(solution)/shard_map/attend/pallas_call | solution.py:366
  248.7 9.7 %all-to-all-start.3 = ((bf16[16,288,128]{2,1,0:T(8,128)(2,1)}), bf16[16,288,128]{2,1,0:T(8,128)(2,1)}, u32[]{:S(2)}, u32[]{:S(2)}) async-start(bf16[16,288,128]{2,1,0:T(8,128)(2,1)} %get-tuple-element.18), calls=%async_computation.3 | async-start | bytes 2359296 | tf_op jit(solution)/shard_map/all_to_all | solution.py:616
  258.5 1.9 collective-permute-start.15
  262.5 1.8 add.124
  264.4 21.6 %collective-permute-done.15.refs_13_ = bf16[1,1024,256]{2,1,0:T(8,128)(2,1)} collective-permute-done((bf16[1,1024,256]{2,1,0:T(8,128)(2,1)S(1)}, bf16[1,1024,256]{2,1,0:T(8,128)(2,1)}, u32[]{:S(2)}, u32[]{:S(2)}) %collective-permute-start.15) | collective-permute-done | bytes 524320 | tf_op jit(solution)/shard_map/ppermute | solution.py:564
  289.7 2.0 collective-permute-start.18
  293.7 3.5 collective-permute-done.1.refs_2_
  298.6 2.2 collective-permute-done.16.refs_14_
  301.6 17.3 %attend_rest.1 = bf16[16,224,128]{2,1,0:T(8,128)(2,1)} custom-call(s32[320]{0:T(512)} %reshape_squeeze.3.pat_ref, s32[16,512]{1,0:T(8,128)} %reshape.140.slot_ref, bf16[16,576,128]{2,1,0:T(8,128)(2,1)} %copy-done, bf16[16,576,128]{2,1,0:T(8,128)(2,1)} %copy-done, bf16[16,576,128]{2,1,0:T(8,128)(2,1)} %copy-done, bf16[512,128]{1,0:T(8,128)(2,1)} %get-tuple-element.15.refs_0_, ...), custom_call_target="tpu_custom_call" | custom-call | tf_op jit(solution)/shard_map/attend_rest/pallas_call | solution.py:366
  318.9 5.4 %all-to-all-start.2 = ((bf16[16,224,128]{2,1,0:T(8,128)(2,1)}), bf16[16,224,128]{2,1,0:T(8,128)(2,1)}, u32[]{:S(2)}, u32[]{:S(2)}) async-start(bf16[16,224,128]{2,1,0:T(8,128)(2,1)} %attend_rest.1), calls=%async_computation.2 | async-start | bytes 1835008 | tf_op jit(solution)/shard_map/all_to_all | solution.py:616
  324.3 1.9 collective-permute-start.7
  326.5 1.9 collective-permute-start.8
  328.3 27.4 %collective-permute-done.7.refs_5_ = bf16[1,1024,256]{2,1,0:T(8,128)(2,1)} collective-permute-done((bf16[1,1024,256]{2,1,0:T(8,128)(2,1)S(1)}, bf16[1,1024,256]{2,1,0:T(8,128)(2,1)}, u32[]{:S(2)}, u32[]{:S(2)}) %collective-permute-start.7) | collective-permute-done | bytes 524320 | tf_op jit(solution)/shard_map/ppermute | solution.py:564
  357.2 9.7 %collective-permute-done.19.refs_18_ = bf16[1,1024,256]{2,1,0:T(8,128)(2,1)S(1)} collective-permute-done((bf16[1,1024,256]{2,1,0:T(8,128)(2,1)S(1)}, bf16[1,1024,256]{2,1,0:T(8,128)(2,1)S(1)}, u32[]{:S(2)}, u32[]{:S(2)}) %collective-permute-start.19) | collective-permute-done | bytes 524320 | tf_op jit(solution)/shard_map/ppermute | solution.py:564
  366.9 2.0 collective-permute-start.22
  371.0 7.1 %collective-permute-done.20.refs_19_ = bf16[1,1024,256]{2,1,0:T(8,128)(2,1)S(1)} collective-permute-done((bf16[1,1024,256]{2,1,0:T(8,128)(2,1)}, bf16[1,1024,256]{2,1,0:T(8,128)(2,1)S(1)}, u32[]{:S(2)}, u32[]{:S(2)}) %collective-permute-start.20) | collective-permute-done | bytes 524320 | tf_op jit(solution)/shard_map/ppermute | solution.py:564
  379.6 5.0 %unpack.1.part_ref = bf16[512,2048]{1,0:T(8,128)(2,1)} custom-call(s32[16,1,512]{2,1,0:T(1,128)} %get-tuple-element.13.order_ref, bf16[16,288,128]{2,1,0:T(8,128)(2,1)} %all-to-all-done.3.in_ref), custom_call_target="tpu_custom_call" | custom-call | tf_op jit(solution)/shard_map/unpack/pallas_call | solution.py:397
  384.6 31.6 %collective-permute-done.9.refs_7_ = bf16[1,1024,256]{2,1,0:T(8,128)(2,1)} collective-permute-done((bf16[1,1024,256]{2,1,0:T(8,128)(2,1)}, bf16[1,1024,256]{2,1,0:T(8,128)(2,1)}, u32[]{:S(2)}, u32[]{:S(2)}) %collective-permute-start.9) | collective-permute-done | bytes 524320 | tf_op jit(solution)/shard_map/ppermute | solution.py:564
  417.2 12.2 %unpack_project.1 = (bf16[512,2048]{1,0:T(8,128)(2,1)}, bf16[512,2048]{1,0:T(8,128)(2,1)}) custom-call(s32[4,8]{1,0:T(4,128)} %get-tuple-element.30.at_ref, s32[16,1,512]{2,1,0:T(1,128)} %get-tuple-element.13.order_ref, bf16[16,224,128]{2,1,0:T(8,128)(2,1)} %all-to-all-done.2.in_ref, bf16[512,2048]{1,0:T(8,128)(2,1)} %unpack.1.part_ref, ...), custom_call_target="tpu_custom_call" | custom-call | tf_op jit(solution)/shard_map/unpack_project/pallas_call | solution.py:526
  429.4 9.2 %project.1 = bf16[512,2048]{1,0:T(8,128)(2,1)S(1)} custom-call(s32[4,8]{1,0:T(4,128)} %get-tuple-element.29.at_ref, bf16[512,2048]{1,0:T(8,128)(2,1)} %get-tuple-element.19.a_ref, bf16[1,1024,256]{2,1,0:T(8,128)(2,1)} %copy-done.4, bf16[1,1024,256]{2,1,0:T(8,128)(2,1)} %collective-permute-done.refs_1_, bf16[1,1024,256]{2,1,0:T(8,128)(2,1)} %copy-done.8, ...), custom_call_target="tpu_custom_call" | custom-call | tf_op jit(solution)/shard_map/project/pallas_call | solution.py:472
  438.6 3.7 add_convert_fusion
  (93 shorter events, 26.4 us)
Async XLA Ops:
  12.1 84.5 %all-to-all-start = ((bf16[16,976,128]{2,1,0:T(8,128)(2,1)}), bf16[16,976,128]{2,1,0:T(8,128)(2,1)}, u32[]{:S(2)}, u32[]{:S(2)}) async-start(bf16[16,976,128]{2,1,0:T(8,128)(2,1)} %get-tuple-element.14), calls=%async_computation | async-start | bytes 7995392 | tf_op jit(solution)/shard_map/all_to_all | solution.py:616
  28.3 87.6 %copy-start.17 = (bf16[2048,256]{1,0:T(8,128)(2,1)S(1)}, bf16[2048,256]{1,0:T(8,128)(2,1)}, u32[]{:S(2)}) copy-start(bf16[2048,256]{1,0:T(8,128)(2,1)} %param.12) | copy-start | bytes 3145732
  96.6 152.1 %all-to-all-start.1 = ((bf16[16,576,128]{2,1,0:T(8,128)(2,1)}), bf16[16,576,128]{2,1,0:T(8,128)(2,1)S(1)}, u32[]{:S(2)}, u32[]{:S(2)}) async-start(bf16[16,576,128]{2,1,0:T(8,128)(2,1)} %pack_rest.1), calls=%async_computation.1 | async-start | bytes 4718592 | tf_op jit(solution)/shard_map/all_to_all | solution.py:616
  115.9 61.9 %collective-permute-start.5 = (bf16[2048,256]{1,0:T(8,128)(2,1)S(1)}, bf16[2048,256]{1,0:T(8,128)(2,1)S(1)}, u32[]{:S(2)}, u32[]{:S(2)}) collective-permute-start(bf16[2048,256]{1,0:T(8,128)(2,1)S(1)} %copy-done.17), channel_id=1, source_target_pairs={{8,0},{10,2},{12,4},{14,6},{16,8},{18,10},{20,12},{22,14},{24,16},... | collective-permute-start | bytes 3145736 | tf_op jit(solution)/shard_map/ppermute | solution.py:564
  117.2 62.9 %collective-permute-start.3 = (bf16[2048,256]{1,0:T(8,128)(2,1)S(1)}, bf16[2048,256]{1,0:T(8,128)(2,1)S(1)}, u32[]{:S(2)}, u32[]{:S(2)}) collective-permute-start(bf16[2048,256]{1,0:T(8,128)(2,1)S(1)} %copy-done.17), channel_id=1, source_target_pairs={{0,8},{2,10},{4,12},{6,14},{8,16},{10,18},{12,20},{14,22},{16,24},... | collective-permute-start | bytes 3145736 | tf_op jit(solution)/shard_map/ppermute | solution.py:564
  178.8 38.7 %collective-permute-start.6 = (bf16[2048,256]{1,0:T(8,128)(2,1)S(1)}, bf16[2048,256]{1,0:T(8,128)(2,1)}, u32[]{:S(2)}, u32[]{:S(2)}) collective-permute-start(bf16[2048,256]{1,0:T(8,128)(2,1)S(1)} %collective-permute-done.5), channel_id=1, source_target_pairs={{8,0},{10,2},{12,4},{14,6},{16,8},{18,10},{20,12},{22,14},{9,1},{1... | collective-permute-start | bytes 3145736 | tf_op jit(solution)/shard_map/ppermute | solution.py:564
  180.1 38.7 %collective-permute-start.4 = (bf16[2048,256]{1,0:T(8,128)(2,1)S(1)}, bf16[2048,256]{1,0:T(8,128)(2,1)}, u32[]{:S(2)}, u32[]{:S(2)}) collective-permute-start(bf16[2048,256]{1,0:T(8,128)(2,1)S(1)} %collective-permute-done.3), channel_id=1, source_target_pairs={{8,16},{10,18},{12,20},{14,22},{16,24},{18,26},{20,28},{22,30},{9,... | collective-permute-start | bytes 3145736 | tf_op jit(solution)/shard_map/ppermute | solution.py:564
  217.5 70.6 %collective-permute-start.10 = (bf16[2048,256]{1,0:T(8,128)(2,1)}, bf16[2048,256]{1,0:T(8,128)(2,1)}, u32[]{:S(2)}, u32[]{:S(2)}) collective-permute-start(bf16[2048,256]{1,0:T(8,128)(2,1)} %collective-permute-done.6), channel_id=1, source_target_pairs={{8,0},{10,2},{12,4},{14,6},{9,1},{11,3},{13,5},{15,7}} | collective-permute-start | bytes 3145736 | tf_op jit(solution)/shard_map/ppermute | solution.py:564
  218.8 70.9 %collective-permute-start.11 = (bf16[2048,256]{1,0:T(8,128)(2,1)}, bf16[2048,256]{1,0:T(8,128)(2,1)}, u32[]{:S(2)}, u32[]{:S(2)}) collective-permute-start(bf16[2048,256]{1,0:T(8,128)(2,1)} %collective-permute-done.4), channel_id=1, source_target_pairs={{16,24},{18,26},{20,28},{22,30},{17,25},{19,27},{21,29},{23,31}} | collective-permute-start | bytes 3145736 | tf_op jit(solution)/shard_map/ppermute | solution.py:564
  248.7 70.2 %all-to-all-start.3 = ((bf16[16,288,128]{2,1,0:T(8,128)(2,1)}), bf16[16,288,128]{2,1,0:T(8,128)(2,1)}, u32[]{:S(2)}, u32[]{:S(2)}) async-start(bf16[16,288,128]{2,1,0:T(8,128)(2,1)} %get-tuple-element.18), calls=%async_computation.3 | async-start | bytes 2359296 | tf_op jit(solution)/shard_map/all_to_all | solution.py:616
  258.5 27.5 %collective-permute-start.15 = (bf16[1,1024,256]{2,1,0:T(8,128)(2,1)S(1)}, bf16[1,1024,256]{2,1,0:T(8,128)(2,1)}, u32[]{:S(2)}, u32[]{:S(2)}) collective-permute-start(bf16[1,1024,256]{2,1,0:T(8,128)(2,1)S(1)} %get-tuple-element.27.refs_12_), channel_id=1, source_target_pairs={{0,2},{2,0},{4,6},{6,4},{8,10},{10,8},{12,14},{14,12},{16,18},{18,... | collective-permute-start | bytes 1572872 | tf_op jit(solution)/shard_map/ppermute | solution.py:564
  260.5 27.0 %collective-permute-start = (bf16[1,1024,256]{2,1,0:T(8,128)(2,1)S(1)}, bf16[1,1024,256]{2,1,0:T(8,128)(2,1)}, u32[]{:S(2)}, u32[]{:S(2)}) collective-permute-start(bf16[1,1024,256]{2,1,0:T(8,128)(2,1)S(1)} %get-tuple-element.28.refs_0_), channel_id=1, source_target_pairs={{0,4},{2,6},{4,0},{6,2},{8,12},{10,14},{12,8},{14,10},{16,20},{18,... | collective-permute-start | bytes 1572872 | tf_op jit(solution)/shard_map/ppermute | solution.py:564
  262.0 35.2 %collective-permute-start.1 = (bf16[1,1024,256]{2,1,0:T(8,128)(2,1)S(1)}, bf16[1,1024,256]{2,1,0:T(8,128)(2,1)S(1)}, u32[]{:S(2)}, u32[]{:S(2)}) collective-permute-start(bf16[1,1024,256]{2,1,0:T(8,128)(2,1)S(1)} %get-tuple-element.28.refs_0_), channel_id=1, source_target_pairs={{0,2},{2,0},{4,6},{6,4},{8,10},{10,8},{12,14},{14,12},{16,18},{18,... | collective-permute-start | bytes 1572872 | tf_op jit(solution)/shard_map/ppermute | solution.py:564
  286.0 14.8 %collective-permute-start.16 = (bf16[1,1024,256]{2,1,0:T(8,128)(2,1)S(1)}, bf16[1,1024,256]{2,1,0:T(8,128)(2,1)S(1)}, u32[]{:S(2)}, u32[]{:S(2)}) collective-permute-start(bf16[1,1024,256]{2,1,0:T(8,128)(2,1)S(1)} %get-tuple-element.27.refs_12_), channel_id=1, source_target_pairs={{0,4},{2,6},{4,0},{6,2},{8,12},{10,14},{12,8},{14,10},{16,20},{18,... | collective-permute-start | bytes 1572872 | tf_op jit(solution)/shard_map/ppermute | solution.py:564
  287.5 36.8 %collective-permute-start.17 = (bf16[1,1024,256]{2,1,0:T(8,128)(2,1)}, bf16[1,1024,256]{2,1,0:T(8,128)(2,1)}, u32[]{:S(2)}, u32[]{:S(2)}) collective-permute-start(bf16[1,1024,256]{2,1,0:T(8,128)(2,1)} %collective-permute-done.15.refs_13_), channel_id=1, source_target_pairs={{0,4},{2,6},{4,0},{6,2},{8,12},{10,14},{12,8},{14,10},{16,20},{18,... | collective-permute-start | bytes 1572872 | tf_op jit(solution)/shard_map/ppermute | solution.py:564
  288.1 38.2 %collective-permute-start.2 = (bf16[1,1024,256]{2,1,0:T(8,128)(2,1)}, bf16[1,1024,256]{2,1,0:T(8,128)(2,1)}, u32[]{:S(2)}, u32[]{:S(2)}) collective-permute-start(bf16[1,1024,256]{2,1,0:T(8,128)(2,1)} %collective-permute-done.refs_1_), channel_id=1, source_target_pairs={{0,2},{2,0},{4,6},{6,4},{8,10},{10,8},{12,14},{14,12},{16,18},{18,... | collective-permute-start | bytes 1572872 | tf_op jit(solution)/shard_map/ppermute | solution.py:564
  289.7 36.8 %collective-permute-start.18 = (bf16[1,1024,256]{2,1,0:T(8,128)(2,1)S(1)}, bf16[1,1024,256]{2,1,0:T(8,128)(2,1)}, u32[]{:S(2)}, u32[]{:S(2)}) collective-permute-start(bf16[1,1024,256]{2,1,0:T(8,128)(2,1)S(1)} %get-tuple-element.25.refs_16_), channel_id=1, source_target_pairs={{0,2},{2,0},{4,6},{6,4},{8,10},{10,8},{12,14},{14,12},{16,18},{18,... | collective-permute-start | bytes 1572872 | tf_op jit(solution)/shard_map/ppermute | solution.py:564
  293.5 73.3 %copy-start.1 = (bf16[2,1024,256]{2,1,0:T(8,128)(2,1)}, bf16[2,1024,256]{2,1,0:T(8,128)(2,1)S(1)}, u32[]{:S(2)}) copy-start(bf16[2,1024,256]{2,1,0:T(8,128)(2,1)S(1)} %pad_maximum_fusion.refs_8_) | copy-start | bytes 3145732
  293.6 73.3 %copy-start.2 = (bf16[2,1024,256]{2,1,0:T(8,128)(2,1)}, bf16[2,1024,256]{2,1,0:T(8,128)(2,1)S(1)}, u32[]{:S(2)}) copy-start(bf16[2,1024,256]{2,1,0:T(8,128)(2,1)S(1)} %pad_maximum_fusion.1.refs_20_) | copy-start | bytes 3145732
  297.2 71.8 %collective-permute-start.12 = (bf16[2,1024,256]{2,1,0:T(8,128)(2,1)S(1)}, bf16[2,1024,256]{2,1,0:T(8,128)(2,1)}, u32[]{:S(2)}, u32[]{:S(2)}) collective-permute-start(bf16[2,1024,256]{2,1,0:T(8,128)(2,1)S(1)} %pad_maximum_fusion.refs_8_), channel_id=1, source_target_pairs={{0,4},{2,6},{4,0},{6,2},{8,12},{10,14},{12,8},{14,10},{16,20},{18,... | collective-permute-start | bytes 3145736 | tf_op jit(solution)/shard_map/ppermute | solution.py:564
  300.8 69.6 %collective-permute-start.21 = (bf16[2,1024,256]{2,1,0:T(8,128)(2,1)S(1)}, bf16[2,1024,256]{2,1,0:T(8,128)(2,1)}, u32[]{:S(2)}, u32[]{:S(2)}) collective-permute-start(bf16[2,1024,256]{2,1,0:T(8,128)(2,1)S(1)} %pad_maximum_fusion.1.refs_20_), channel_id=1, source_target_pairs={{0,2},{2,0},{4,6},{6,4},{8,10},{10,8},{12,14},{14,12},{16,18},{18,... | collective-permute-start | bytes 3145736 | tf_op jit(solution)/shard_map/ppermute | solution.py:564
  318.9 97.4 %all-to-all-start.2 = ((bf16[16,224,128]{2,1,0:T(8,128)(2,1)}), bf16[16,224,128]{2,1,0:T(8,128)(2,1)}, u32[]{:S(2)}, u32[]{:S(2)}) async-start(bf16[16,224,128]{2,1,0:T(8,128)(2,1)} %attend_rest.1), calls=%async_computation.2 | async-start | bytes 1835008 | tf_op jit(solution)/shard_map/all_to_all | solution.py:616
  324.3 31.4 %collective-permute-start.7 = (bf16[1,1024,256]{2,1,0:T(8,128)(2,1)S(1)}, bf16[1,1024,256]{2,1,0:T(8,128)(2,1)}, u32[]{:S(2)}, u32[]{:S(2)}) collective-permute-start(bf16[1,1024,256]{2,1,0:T(8,128)(2,1)S(1)} %get-tuple-element.26.refs_4_), channel_id=1, source_target_pairs={{0,4},{2,6},{4,0},{6,2},{8,12},{10,14},{12,8},{14,10},{16,20},{18,... | collective-permute-start | bytes 1572872 | tf_op jit(solution)/shard_map/ppermute | solution.py:564
  326.3 40.6 %collective-permute-start.19 = (bf16[1,1024,256]{2,1,0:T(8,128)(2,1)S(1)}, bf16[1,1024,256]{2,1,0:T(8,128)(2,1)S(1)}, u32[]{:S(2)}, u32[]{:S(2)}) collective-permute-start(bf16[1,1024,256]{2,1,0:T(8,128)(2,1)S(1)} %get-tuple-element.25.refs_16_), channel_id=1, source_target_pairs={{0,4},{2,6},{4,0},{6,2},{8,12},{10,14},{12,8},{14,10},{16,20},{18,... | collective-permute-start | bytes 1572872 | tf_op jit(solution)/shard_map/ppermute | solution.py:564
  326.5 40.4 %collective-permute-start.8 = (bf16[1,1024,256]{2,1,0:T(8,128)(2,1)S(1)}, bf16[1,1024,256]{2,1,0:T(8,128)(2,1)S(1)}, u32[]{:S(2)}, u32[]{:S(2)}) collective-permute-start(bf16[1,1024,256]{2,1,0:T(8,128)(2,1)S(1)} %get-tuple-element.26.refs_4_), channel_id=1, source_target_pairs={{0,2},{2,0},{4,6},{6,4},{8,10},{10,8},{12,14},{14,12},{16,18},{18,... | collective-permute-start | bytes 1572872 | tf_op jit(solution)/shard_map/ppermute | solution.py:564
  355.7 22.4 %collective-permute-start.20 = (bf16[1,1024,256]{2,1,0:T(8,128)(2,1)}, bf16[1,1024,256]{2,1,0:T(8,128)(2,1)S(1)}, u32[]{:S(2)}, u32[]{:S(2)}) collective-permute-start(bf16[1,1024,256]{2,1,0:T(8,128)(2,1)} %collective-permute-done.18.refs_17_), channel_id=1, source_target_pairs={{0,4},{2,6},{4,0},{6,2},{8,12},{10,14},{12,8},{14,10},{16,20},{18,... | collective-permute-start | bytes 1572872 | tf_op jit(solution)/shard_map/ppermute | solution.py:564
  366.8 49.3 %collective-permute-start.13 = (bf16[2,1024,256]{2,1,0:T(8,128)(2,1)S(1)}, bf16[2,1024,256]{2,1,0:T(8,128)(2,1)}, u32[]{:S(2)}, u32[]{:S(2)}) collective-permute-start(bf16[2,1024,256]{2,1,0:T(8,128)(2,1)S(1)} %pad_maximum_fusion.refs_8_), channel_id=1, source_target_pairs={{0,2},{2,0},{4,6},{6,4},{8,10},{10,8},{12,14},{14,12},{16,18},{18,... | collective-permute-start | bytes 3145736 | tf_op jit(solution)/shard_map/ppermute | solution.py:564
  366.9 49.3 %collective-permute-start.22 = (bf16[2,1024,256]{2,1,0:T(8,128)(2,1)S(1)}, bf16[2,1024,256]{2,1,0:T(8,128)(2,1)S(1)}, u32[]{:S(2)}, u32[]{:S(2)}) collective-permute-start(bf16[2,1024,256]{2,1,0:T(8,128)(2,1)S(1)} %pad_maximum_fusion.1.refs_20_), channel_id=1, source_target_pairs={{0,4},{2,6},{4,0},{6,2},{8,12},{10,14},{12,8},{14,10},{16,20},{18,... | collective-permute-start | bytes 3145736 | tf_op jit(solution)/shard_map/ppermute | solution.py:564
  368.9 47.3 %collective-permute-start.14 = (bf16[2,1024,256]{2,1,0:T(8,128)(2,1)}, bf16[2,1024,256]{2,1,0:T(8,128)(2,1)}, u32[]{:S(2)}, u32[]{:S(2)}) collective-permute-start(bf16[2,1024,256]{2,1,0:T(8,128)(2,1)} %collective-permute-done.12.refs_9_), channel_id=1, source_target_pairs={{0,2},{2,0},{4,6},{6,4},{8,10},{10,8},{12,14},{14,12},{16,18},{18,... | collective-permute-start | bytes 3145736 | tf_op jit(solution)/shard_map/ppermute | solution.py:564
  370.4 45.9 %collective-permute-start.23 = (bf16[2,1024,256]{2,1,0:T(8,128)(2,1)}, bf16[2,1024,256]{2,1,0:T(8,128)(2,1)}, u32[]{:S(2)}, u32[]{:S(2)}) collective-permute-start(bf16[2,1024,256]{2,1,0:T(8,128)(2,1)} %collective-permute-done.21.refs_21_), channel_id=1, source_target_pairs={{0,4},{2,6},{4,0},{6,2},{8,12},{10,14},{12,8},{14,10},{16,20},{18,... | collective-permute-start | bytes 3145736 | tf_op jit(solution)/shard_map/ppermute | solution.py:564
  378.9 37.3 %collective-permute-start.9 = (bf16[1,1024,256]{2,1,0:T(8,128)(2,1)}, bf16[1,1024,256]{2,1,0:T(8,128)(2,1)}, u32[]{:S(2)}, u32[]{:S(2)}) collective-permute-start(bf16[1,1024,256]{2,1,0:T(8,128)(2,1)} %collective-permute-done.7.refs_5_), channel_id=1, source_target_pairs={{0,2},{2,0},{4,6},{6,4},{8,10},{10,8},{12,14},{14,12},{16,18},{18,... | collective-permute-start | bytes 1572872 | tf_op jit(solution)/shard_map/ppermute | solution.py:564
  429.4 9.2 %collective-permute-start.24 = (bf16[512,2048]{1,0:T(8,128)(2,1)}, bf16[512,2048]{1,0:T(8,128)(2,1)}, u32[]{:S(2)}, u32[]{:S(2)}) collective-permute-start(bf16[512,2048]{1,0:T(8,128)(2,1)} %get-tuple-element.20), channel_id=1, source_target_pairs={{0,1},{1,0},{2,3},{3,2},{4,5},{5,4},{6,7},{7,6},{8,9},{9,8},{10,11... | collective-permute-start | bytes 6291464 | tf_op jit(solution)/shard_map/ppermute | solution.py:638
  (15 other events, 274.3 us)
